TPU v7x, 32 devices: a whole 2x2x4 slice. The times are simulated.
32 devices in a mesh: ex: 2 (over core), ey: 16 (over z, y, x).
Axes of the slice: x: 2, y: 2, z: 4, core: 2. Of those that a mesh axis runs over, the one named last changes fastest.
Arguments:
- tokens: bfloat16 [32, 256, 1024], P(('ex', 'ey')), may hold values from -16 to 16
- slot_param: bfloat16 [1024, 32], replicated, may hold values from -0.75 to 0.75
- weight_in: bfloat16 [32, 1024, 4096], P('ey', None, 'ex'), may hold values from -0.1875 to 0.1875
- weight_out: bfloat16 [32, 4096, 1024], P('ey', 'ex'), may hold values from -0.09375 to 0.09375
- grad_out: bfloat16 [32, 256, 1024], P(('ex', 'ey')), may hold values from -6 to 6
Outputs:
- grad_tokens: bfloat16 [32, 256, 1024], P(('ex', 'ey'))
- grad_param: float32 [1024, 32], replicated
- grad_win: bfloat16 [32, 1024, 4096], P('ey', None, 'ex')
- grad_wout: bfloat16 [32, 4096, 1024], P('ey', 'ex')
All inputs are finite; a program needn't handle non-finite values.
Results may differ from a plain program's by a relative error of at most 0.017.
Values may be sent and summed in bfloat16 or wider, within the bound.
No kernel may reach another device: no remote copies, remote signals or barrier semaphores. Data moves between devices by JAX's collectives and lax.ppermute only.
A program may use at most 64 MiB of HBM per device.

v0:
```python
import jax
import jax.numpy as jnp
from jax import lax
from jax.sharding import PartitionSpec as P


def gelu_parts(pre):
    cdf = 0.5 * (1.0 + lax.erf(pre * 0.7071067811865476))
    slope = cdf + pre * jnp.exp(-0.5 * pre * pre) * 0.3989422804014327
    return (pre * cdf, slope)


def softmax_along(values, axis):
    top = jnp.max(values, axis=axis, keepdims=True)
    expo = jnp.exp(values - top)
    return expo / jnp.sum(expo, axis=axis, keepdims=True)


def route_in(stacked):
    moved = lax.all_to_all(stacked, "ey", split_axis=2, concat_axis=0, tiled=True)
    return lax.all_gather(moved, "ex", axis=0, tiled=True)


def route_out(term_fn, total_rows):
    summed = lax.psum_scatter(
        term_fn(jnp.int32(0), total_rows // lax.axis_size("ex") * lax.axis_size("ex")).astype(
            jnp.bfloat16
        ),
        "ex",
        scatter_dimension=0,
        tiled=True,
    )
    return lax.all_to_all(summed, "ey", split_axis=0, concat_axis=2, tiled=True)


def per_device(tokens, slot_param, weight_in, weight_out, grad_out):
    logits = jnp.einsum("ipd,ds->ips", tokens, slot_param, preferred_element_type=jnp.float32)
    dispatch = softmax_along(logits, 1)
    combine = softmax_along(logits, 2)
    dispatch_b = dispatch.astype(jnp.bfloat16)
    combine_b = combine.astype(jnp.bfloat16)
    slot_in = jnp.einsum(
        "ips,ipd->isd", dispatch_b, tokens, preferred_element_type=jnp.float32
    ).astype(jnp.bfloat16)
    slot_cot = jnp.einsum(
        "ips,ipd->isd", combine_b, grad_out, preferred_element_type=jnp.float32
    ).astype(jnp.bfloat16)
    arrived = route_in(jnp.stack((slot_in, slot_cot), axis=1))
    total_rows = arrived.shape[0]
    slot_x = arrived[:, 0]
    slot_g = arrived[:, 1]
    pre = jnp.einsum("red,edf->ref", slot_x, weight_in, preferred_element_type=jnp.float32)
    value, slope = gelu_parts(pre)
    hidden = value.astype(jnp.bfloat16)
    back = jnp.einsum("red,efd->ref", slot_g, weight_out, preferred_element_type=jnp.float32)
    dpre = (back * slope).astype(jnp.bfloat16)

    def paired_term(start, count):
        return jnp.concatenate(
            (
                jnp.einsum("ref,efd->red", hidden, weight_out, preferred_element_type=jnp.float32)[
                    :, None
                ],
                jnp.einsum("ref,edf->red", dpre, weight_in, preferred_element_type=jnp.float32)[
                    :, None
                ],
            ),
            axis=1,
        )

    paired = route_out(paired_term, total_rows)
    slot_out = paired[:, 0]
    grad_slot = paired[:, 1]
    grad_win = jnp.einsum("red,ref->edf", slot_x, dpre, preferred_element_type=jnp.float32).astype(
        jnp.bfloat16
    )
    grad_wout = jnp.einsum(
        "ref,red->efd", hidden, slot_g, preferred_element_type=jnp.float32
    ).astype(jnp.bfloat16)
    d_combine = jnp.einsum("ipd,isd->ips", grad_out, slot_out, preferred_element_type=jnp.float32)
    d_dispatch = jnp.einsum("ipd,isd->ips", tokens, grad_slot, preferred_element_type=jnp.float32)
    d_logits = dispatch * (d_dispatch - jnp.sum(dispatch * d_dispatch, axis=1, keepdims=True))
    d_logits = d_logits + combine * (
        d_combine - jnp.sum(combine * d_combine, axis=2, keepdims=True)
    )
    logit_grad = d_logits.astype(jnp.bfloat16)
    grad_tokens = jnp.einsum(
        "ips,isd->ipd", dispatch_b, grad_slot, preferred_element_type=jnp.float32
    )
    grad_tokens = grad_tokens + jnp.einsum(
        "ips,ds->ipd", logit_grad, slot_param, preferred_element_type=jnp.float32
    )
    local_param = jnp.einsum("ipd,ips->ds", tokens, logit_grad, preferred_element_type=jnp.float32)
    grad_param = lax.psum(local_param, ("ex", "ey"))
    return (grad_tokens.astype(jnp.bfloat16), grad_param, grad_win, grad_wout)


def solution(mesh):
    in_specs = (
        P(("ex", "ey"), None, None),
        P(),
        P("ey", None, "ex"),
        P("ey", "ex", None),
        P(("ex", "ey"), None, None),
    )
    out_specs = (P(("ex", "ey"), None, None), P(), P("ey", None, "ex"), P("ey", "ex", None))
    return jax.shard_map(
        per_device, mesh=mesh, in_specs=in_specs, out_specs=out_specs, check_vma=False
    )
```

profile of v0, /device:TPU:0, one launch (start us, length us, event | category | flops | bytes accessed | tf_op | source)
XLA Modules:
  0.0 198.2 jit_solution(10697608207090606354)
XLA Ops:
  7.2 1.0 copy-done
  8.2 1.2 fusion.36
  9.6 0.2 fusion.6
  9.9 1.2 fusion.7
  11.3 15.9 %all_to_all.36 = bf16[1,2,32,1024]{3,1,0,2:T(2,128)(2,1)S(1)} all-to-all(bf16[1,2,32,1024]{3,1,0,2:T(2,128)(2,1)S(1)} %copy.17), channel_id=1, replica_groups=mesh['ex'=2,'ey'=16] {'ey'}, dimensions={2} | all-to-all | bytes 262144 | tf_op jit(solution)/shard_map/all_to_all | solution.py:20
  27.3 2.1 %all-gather = bf16[32,1,2,2,1024]{4,0,3,2,1:T(8,128)(2,1)S(1)} all-gather(bf16[16,1,2,2,1024]{4,0,3,2,1:T(8,128)(2,1)S(1)} %bitcast.90), channel_id=2, replica_groups=mesh['ex'=2,'ey'=16] {'ex'}, dimensions={0}, use_global_device_ids=true | all-gather | bytes 393216 | tf_op jit(solution)/shard_map/all_gather | solution.py:21
  29.4 5.1 %convolution_bitcast_fusion.1 = f32[32,2,2048]{2,0,1:T(8,128)S(1)} fusion(bf16[2,1024,2048]{2,1,0:T(8,128)(2,1)} %param.7, bf16[32,2,2,1024]{3,0,2,1:T(8,128)(2,1)S(1)} %bitcast.85), kind=kOutput, calls=%fused_computation.4 | convolution fusion | flops 268435456 | bytes 9043968 | tf_op jit(solution)/shard_map/red,edf->ref/dot_general | solution.py:52
  34.5 1.5 fusion.4
  36.0 2.6 %fusion.1 = bf16[32,2,2048]{2,0,1:T(8,128)(2,1)S(1)} fusion(bf16[2,2048,1024]{2,1,0:T(8,128)(2,1)S(1)} %bitcast.82, f32[32,2,2048]{2,0,1:T(8,128)S(1)} %convolution_bitcast_fusion.1, bf16[32,2,2,1024]{3,0,2,1:T(8,128)(2,1)S(1)} %bitcast.86), kind=kOutput, calls=%fused_computation.5 | convolution fusion | flops 269746176 | bytes 9306112 | tf_op jit(solution)/shard_map/red,efd->ref/dot_general | solution.py:55
  38.7 2.6 %fusion.5 = bf16[32,1,2,1024]{3,0,2,1:T(8,128)(2,1)S(1)} fusion(bf16[32,2,2048]{2,0,1:T(8,128)(2,1)S(1)} %fusion.1, bf16[2,1024,2048]{2,1,0:T(8,128)(2,1)S(1)} %bitcast.84), kind=kOutput, calls=%fused_computation.12 | convolution fusion | flops 268500992 | bytes 8781824 | tf_op jit(solution)/shard_map/ref,edf->red/dot_general | solution.py:64
  41.2 0.7 pad_maximum_fusion
  42.0 5.8 %convolution_convert_fusion = bf16[2,2048,1024]{2,1,0:T(8,128)(2,1)} fusion(bf16[32,2,2,1024]{3,0,2,1:T(8,128)(2,1)S(1)} %bitcast.87, f32[32,2,2048]{2,0,1:T(8,128)S(1)} %convolution_bitcast_fusion.1), kind=kOutput, calls=%fused_computation | convolution fusion | flops 273285120 | bytes 9043968 | tf_op jit(solution)/shard_map/ref,red->efd/dot_general | solution.py:77
  47.8 1.7 copy.19
  49.5 6.0 %all-to-all-start.1 = ((bf16[16,2,2,1024]{3,2,1,0:T(2,128)(2,1)}), bf16[16,2,2,1024]{3,2,1,0:T(2,128)(2,1)S(1)}, u32[]{:S(2)}, u32[]{:S(2)}) async-start(bf16[16,2,2,1024]{3,2,1,0:T(2,128)(2,1)} %copy.19), calls=%async_computation.2 | async-start | bytes 262144 | tf_op jit(solution)/shard_map/all_to_all | solution.py:33
  55.5 0.2 all-reduce.2.cloned.1.call-start
  55.8 5.8 %convolution_convert_fusion.1 = bf16[2,1024,2048]{2,1,0:T(8,128)(2,1)} fusion(bf16[32,2,2048]{2,0,1:T(8,128)(2,1)S(1)} %fusion.1, bf16[32,2,2,1024]{3,0,2,1:T(8,128)(2,1)S(1)} %bitcast.88), kind=kOutput, calls=%fused_computation.1 | convolution fusion | flops 272629760 | bytes 8781824 | tf_op jit(solution)/shard_map/red,ref->edf/dot_general | solution.py:74
  61.6 1.9 all-to-all-done.1
  63.8 0.3 convolution_bitcast_fusion.3
  64.1 0.4 fusion.22
  64.5 0.4 multiply_reduce_fusion.1
  64.8 0.9 convolution_bitcast_fusion.2
  65.8 1.2 fusion.3
  67.0 122.8 %all-reduce.2.cloned.1.call-done = f32[1024,32]{0,1:T(8,128)} async-done(((f32[1024,32]{0,1:T(8,128)}), f32[1024,32]{0,1:T(8,128)}) %all-reduce.2.cloned.1.call-update) | async-done | bytes 131088 | tf_op jit(solution)/shard_map/psum | solution.py:94
  189.8 1.6 copy.40
  (25 shorter events, 0.8 us)
Async XLA Ops:
  7.2 1.0 copy-start
  7.2 40.6 %reduce-scatter.2.cloned.1.call-start = ((), (), s32[]{:S(2)}) async-start(), calls=%async_computation.3 | async-start | bytes 393216 | tf_op jit(solution)/shard_map/reduce_scatter | solution.py:25
  27.2 7.3 %slice-start = ((s8[8388608]{0:T(1024)(128)(4,1)}), s8[4194304]{0:T(1024)(128)(4,1)S(1)}, s32[]{:S(2)}) async-start(s8[8388608]{0:T(1024)(128)(4,1)} %bitcast.81), calls=%async_computation.5 | async-start | bytes 8388608
  29.4 5.1 %slice-start.1 = ((s8[8388608]{0:T(1024)(128)(4,1)}), s8[4194304]{0:T(1024)(128)(4,1)S(1)}, s32[]{:S(2)}) async-start(s8[8388608]{0:T(1024)(128)(4,1)} %bitcast.81), calls=%async_computation.6 | async-start | bytes 8388608
  29.4 9.3 %slice-start.2 = ((s8[8388608]{0:T(1024)(128)(4,1)}), s8[4194304]{0:T(1024)(128)(4,1)S(1)}, s32[]{:S(2)}) async-start(s8[8388608]{0:T(1024)(128)(4,1)} %bitcast.83), calls=%async_computation.7 | async-start | bytes 8388608
  34.5 4.2 %slice-start.3 = ((s8[8388608]{0:T(1024)(128)(4,1)}), s8[4194304]{0:T(1024)(128)(4,1)S(1)}, s32[]{:S(2)}) async-start(s8[8388608]{0:T(1024)(128)(4,1)} %bitcast.83), calls=%async_computation.8 | async-start | bytes 8388608
  42.0 21.8 %copy-start.1 = (bf16[1,256,1024]{2,1,0:T(8,128)(2,1)S(1)}, bf16[1,256,1024]{2,1,0:T(8,128)(2,1)}, u32[]{:S(2)}) copy-start(bf16[1,256,1024]{2,1,0:T(8,128)(2,1)} %param.9) | copy-start | bytes 1572868
  47.8 18.0 %copy-start.2 = (bf16[1024,32]{0,1:T(8,128)(2,1)S(1)}, bf16[1024,32]{0,1:T(8,128)(2,1)}, u32[]{:S(2)}) copy-start(bf16[1024,32]{0,1:T(8,128)(2,1)} %param.6) | copy-start | bytes 196612
  49.5 13.9 %all-to-all-start.1 = ((bf16[16,2,2,1024]{3,2,1,0:T(2,128)(2,1)}), bf16[16,2,2,1024]{3,2,1,0:T(2,128)(2,1)S(1)}, u32[]{:S(2)}, u32[]{:S(2)}) async-start(bf16[16,2,2,1024]{3,2,1,0:T(2,128)(2,1)} %copy.19), calls=%async_computation.2 | async-start | bytes 262144 | tf_op jit(solution)/shard_map/all_to_all | solution.py:33
  55.5 134.3 %all-reduce.2.cloned.1.call-start = ((), (), s32[]{:S(2)}) async-start(), calls=%async_computation.4 | async-start | bytes 262144 | tf_op jit(solution)/shard_map/psum | solution.py:94
Sparse Core Ops, SparseCore 0:
  42.1 4.9 reduce-scatter.1
  65.9 123.8 all-reduce.1
where the time goes:
time: 199 us; the launch traced here: 198 us
  waiting for transfers between devices  125 us (63%)
  matrix products  29.2 us (15%)
  blocking collectives  18.1 us (9%)
  between operations  14.2 us (7%)
  starting transfers between devices  6.26 us (3%)
  local copies, waits for them, and re-layouts  4.79 us (2%)
    psum x1, waiting for transfers between devices, per_device(): grad_param = lax.psum(local_param, ('ex', 'ey'))  123 us
    all_to_all x1, blocking collectives, route_in(): lax.all_to_all(stacked, 'ey', split_axis=2, concat_axis=0, tiled=True)  15.9 us
    all_to_all x1, starting transfers between devices, route_out(): return lax.all_to_all(summed, 'ey', split_axis=0, concat_axis=2, tiled=True)  6 us
    dot_general x1, matrix products, per_device(): jnp.einsum('ref,red->efd', hidden, slot_g, preferred_element_type=jnp.flo...  5.78 us
    dot_general x1, matrix products, per_device(): jnp.einsum('red,ref->edf', slot_x, dpre, preferred_element_type=jnp.float32)  5.78 us
    dot_general x1, matrix products, per_device(): jnp.einsum('red,edf->ref', slot_x, weight_in, preferred_element_type=jnp....  5.07 us
  transfers between devices with their start and end apart: 3, of which 2 were waited for; matrix products, arithmetic and copies ran while one was open for 6% of the time, Pallas kernels for 0%

commit v1 on v0

--- a/solution.py
+++ b/solution.py
@@ -91,7 +91,7 @@
         "ips,ds->ipd", logit_grad, slot_param, preferred_element_type=jnp.float32
     )
     local_param = jnp.einsum("ipd,ips->ds", tokens, logit_grad, preferred_element_type=jnp.float32)
-    grad_param = lax.psum(local_param, ("ex", "ey"))
+    grad_param = jax.lax.all_gather(local_param, axis_name=("ex", "ey")).sum(axis=0)
     return (grad_tokens.astype(jnp.bfloat16), grad_param, grad_win, grad_wout)
 
 

time: 199 us -> 138 us (0.69)
  waiting for transfers between devices: 125 us -> 52 us
  blocking collectives: 18.1 us -> 32.5 us
  starting transfers between devices: 6.26 us -> 0.08 us
  local copies, waits for them, and re-layouts: 4.79 us -> 7.16 us
    psum x1 -> x0, waiting for transfers between devices: 123 us -> none  [per_device(): grad_param = lax.psum(local_param, ('ex', 'ey'))]
    all_gather x0 -> x1, waiting for transfers between devices: none -> 47 us  [per_device(): jax.lax.all_gather(local_param, axis_name=('ex', 'ey')).sum(axis=0)]
    all_to_all x0 -> x1, blocking collectives: none -> 14.5 us  [route_out(): return lax.all_to_all(summed, 'ey', split_axis=0, concat_axis=2, tiled=True)]
    all_to_all x1 -> x0, starting transfers between devices: 6 us -> none  [route_out(): return lax.all_to_all(summed, 'ey', split_axis=0, concat_axis=2, tiled=True)]
    reduce_scatter x1, waiting for transfers between devices: 0.01 us -> 5.05 us  [route_out(): lax.psum_scatter(term_fn(jnp.int32(0), total_rows // lax.axis_size('ex')...]
    unnamed x15, local copies, waits for them, and re-layouts: 2.6 us -> 5.65 us
  transfers between devices with their start and end apart: 3 -> 2, of which waited for: 2 -> 2; matrix products, arithmetic and copies ran while one was open for 6% -> 10% of each run, Pallas kernels for 0% -> 0%
where the time goes in v1:
time: 138 us; the launch traced here: 137 us
  waiting for transfers between devices  52 us (38%)
  blocking collectives  32.5 us (24%)
  matrix products  29.2 us (21%)
  between operations  14.2 us (10%)
  local copies, waits for them, and re-layouts  7.16 us (5%)
  other arithmetic  2.23 us (2%)
    all_gather x1, waiting for transfers between devices, per_device(): jax.lax.all_gather(local_param, axis_name=('ex', 'ey')).sum(axis=0)  47 us
    all_to_all x1, blocking collectives, route_in(): lax.all_to_all(stacked, 'ey', split_axis=2, concat_axis=0, tiled=True)  15.9 us
    all_to_all x1, blocking collectives, route_out(): return lax.all_to_all(summed, 'ey', split_axis=0, concat_axis=2, tiled=True)  14.5 us
    dot_general x1, matrix products, per_device(): jnp.einsum('ref,red->efd', hidden, slot_g, preferred_element_type=jnp.flo...  5.78 us
    dot_general x1, matrix products, per_device(): jnp.einsum('red,ref->edf', slot_x, dpre, preferred_element_type=jnp.float32)  5.78 us
    unnamed x15, local copies, waits for them, and re-layouts  5.65 us
    dot_general x1, matrix products, per_device(): jnp.einsum('red,edf->ref', slot_x, weight_in, preferred_element_type=jnp....  5.07 us
    reduce_scatter x1, waiting for transfers between devices, route_out(): lax.psum_scatter(term_fn(jnp.int32(0), total_rows // lax.axis_size('ex')...  5.05 us
  transfers between devices with their start and end apart: 2, of which 2 were waited for; matrix products, arithmetic and copies ran while one was open for 10% of the time, Pallas kernels for 0%

profile of v1, /device:TPU:0, one launch (start us, length us, event | category | flops | bytes accessed | tf_op | source)
XLA Modules:
  0.0 137.4 jit_solution(2617413617621177154)
XLA Ops:
  7.2 1.0 copy-done
  8.2 1.2 fusion.36
  9.6 0.2 fusion.6
  9.9 1.2 fusion.7
  11.3 15.9 %all_to_all.36 = bf16[1,2,32,1024]{3,1,0,2:T(2,128)(2,1)S(1)} all-to-all(bf16[1,2,32,1024]{3,1,0,2:T(2,128)(2,1)S(1)} %copy.17), channel_id=1, replica_groups=mesh['ex'=2,'ey'=16] {'ey'}, dimensions={2} | all-to-all | bytes 262144 | tf_op jit(solution)/shard_map/all_to_all | solution.py:20
  27.3 2.1 %all-gather = bf16[32,1,2,2,1024]{4,0,3,2,1:T(8,128)(2,1)S(1)} all-gather(bf16[16,1,2,2,1024]{4,0,3,2,1:T(8,128)(2,1)S(1)} %bitcast.96), channel_id=2, replica_groups=mesh['ex'=2,'ey'=16] {'ex'}, dimensions={0}, use_global_device_ids=true | all-gather | bytes 393216 | tf_op jit(solution)/shard_map/all_gather | solution.py:21
  29.4 5.1 %convolution_bitcast_fusion.1 = f32[32,2,2048]{2,0,1:T(8,128)S(1)} fusion(bf16[2,1024,2048]{2,1,0:T(8,128)(2,1)} %param.7, bf16[32,2,2,1024]{3,0,2,1:T(8,128)(2,1)S(1)} %bitcast.90), kind=kOutput, calls=%fused_computation.5 | convolution fusion | flops 268435456 | bytes 9043968 | tf_op jit(solution)/shard_map/red,edf->ref/dot_general | solution.py:52
  34.5 1.5 %fusion.4 = bf16[32,1,2,1024]{3,0,2,1:T(8,128)(2,1)S(1)} fusion(bf16[2,2048,1024]{2,1,0:T(8,128)(2,1)S(1)} %bitcast.87, f32[32,2,2048]{2,0,1:T(8,128)S(1)} %convolution_bitcast_fusion.1), kind=kOutput, calls=%fused_computation.12 | convolution fusion | flops 269156352 | bytes 9043968 | tf_op jit(solution)/shard_map/ref,efd->red/dot_general | solution.py:61
  36.1 2.6 %fusion.1 = bf16[32,2,2048]{2,0,1:T(8,128)(2,1)S(1)} fusion(bf16[2,2048,1024]{2,1,0:T(8,128)(2,1)S(1)} %bitcast.87, f32[32,2,2048]{2,0,1:T(8,128)S(1)} %convolution_bitcast_fusion.1, bf16[32,2,2,1024]{3,0,2,1:T(8,128)(2,1)S(1)} %bitcast.91), kind=kOutput, calls=%fused_computation.6 | convolution fusion | flops 269746176 | bytes 9306112 | tf_op jit(solution)/shard_map/red,efd->ref/dot_general | solution.py:55
  38.7 2.6 %fusion.5 = bf16[32,1,2,1024]{3,0,2,1:T(8,128)(2,1)S(1)} fusion(bf16[32,2,2048]{2,0,1:T(8,128)(2,1)S(1)} %fusion.1, bf16[2,1024,2048]{2,1,0:T(8,128)(2,1)S(1)} %bitcast.89), kind=kOutput, calls=%fused_computation.13 | convolution fusion | flops 268500992 | bytes 8781824 | tf_op jit(solution)/shard_map/ref,edf->red/dot_general | solution.py:64
  41.2 0.7 pad_maximum_fusion
  42.1 5.0 %reduce-scatter.2.cloned.1.call-done = bf16[16,2,2,1024]{3,0,2,1:T(8,128)(2,1)} async-done(((bf16[32,2,2,1024]{3,0,2,1:T(8,128)(2,1)}), bf16[16,2,2,1024]{3,0,2,1:T(8,128)(2,1)}) %reduce-scatter.2.cloned.1.call-update) | async-done | bytes 131088 | tf_op jit(solution)/shard_map/reduce_scatter | solution.py:25
  47.1 1.0 copy.19
  48.2 14.5 %all_to_all.37 = bf16[16,2,2,1024]{3,2,1,0:T(2,128)(2,1)S(1)} all-to-all(bf16[16,2,2,1024]{3,2,1,0:T(2,128)(2,1)S(1)} %copy.19), channel_id=1, replica_groups=mesh['ex'=2,'ey'=16] {'ey'}, dimensions={0} | all-to-all | bytes 262144 | tf_op jit(solution)/shard_map/all_to_all | solution.py:33
  62.9 0.3 convolution_bitcast_fusion.3
  63.2 0.4 multiply_reduce_fusion.1
  63.6 0.9 convolution_bitcast_fusion.2
  64.5 5.8 %convolution_convert_fusion.1 = bf16[2,1024,2048]{2,1,0:T(8,128)(2,1)} fusion(bf16[32,2,2048]{2,0,1:T(8,128)(2,1)S(1)} %fusion.1, bf16[32,2,2,1024]{3,0,2,1:T(8,128)(2,1)S(1)} %bitcast.92), kind=kOutput, calls=%fused_computation.1 | convolution fusion | flops 272629760 | bytes 8781824 | tf_op jit(solution)/shard_map/red,ref->edf/dot_general | solution.py:74
  70.3 5.8 %convolution_convert_fusion = bf16[2,2048,1024]{2,1,0:T(8,128)(2,1)} fusion(bf16[32,2,2,1024]{3,0,2,1:T(8,128)(2,1)S(1)} %bitcast.93, f32[32,2,2048]{2,0,1:T(8,128)S(1)} %convolution_bitcast_fusion.1), kind=kOutput, calls=%fused_computation | convolution fusion | flops 273285120 | bytes 9043968 | tf_op jit(solution)/shard_map/ref,red->efd/dot_general | solution.py:77
  76.1 0.4 fusion.22
  76.5 1.2 fusion.3
  77.7 47.0 %all-gather.4.cloned.1.call-done = f32[32768,32]{0,1:T(8,128)} async-done(((f32[1024,32]{0,1:T(8,128)}), f32[32768,32]{0,1:T(8,128)}) %all-gather.4.cloned.1.call-update) | async-done | bytes 4194320 | tf_op jit(solution)/shard_map/all_gather | solution.py:94
  124.7 4.6 %copy.23 = f32[4,8,32,1024]{3,2,1,0:T(8,128)S(1)} copy(f32[4,8,32,1024]{3,1,2,0:T(8,128)} %bitcast.94) | data formatting | bytes 8388608
  129.3 1.3 bitcast_reduce_fusion
  (25 shorter events, 0.8 us)
Async XLA Ops:
  7.2 1.0 copy-start
  7.2 39.9 %reduce-scatter.2.cloned.1.call-start = ((), (), s32[]{:S(2)}) async-start(), calls=%async_computation.3 | async-start | bytes 393216 | tf_op jit(solution)/shard_map/reduce_scatter | solution.py:25
  27.2 7.3 %slice-start = ((s8[8388608]{0:T(1024)(128)(4,1)}), s8[4194304]{0:T(1024)(128)(4,1)S(1)}, s32[]{:S(2)}) async-start(s8[8388608]{0:T(1024)(128)(4,1)} %bitcast.86), calls=%async_computation.5 | async-start | bytes 8388608
  29.4 5.1 %slice-start.1 = ((s8[8388608]{0:T(1024)(128)(4,1)}), s8[4194304]{0:T(1024)(128)(4,1)S(1)}, s32[]{:S(2)}) async-start(s8[8388608]{0:T(1024)(128)(4,1)} %bitcast.86), calls=%async_computation.6 | async-start | bytes 8388608
  29.4 9.3 %slice-start.2 = ((s8[8388608]{0:T(1024)(128)(4,1)}), s8[4194304]{0:T(1024)(128)(4,1)S(1)}, s32[]{:S(2)}) async-start(s8[8388608]{0:T(1024)(128)(4,1)} %bitcast.88), calls=%async_computation.7 | async-start | bytes 8388608
  34.5 4.2 %slice-start.3 = ((s8[8388608]{0:T(1024)(128)(4,1)}), s8[4194304]{0:T(1024)(128)(4,1)S(1)}, s32[]{:S(2)}) async-start(s8[8388608]{0:T(1024)(128)(4,1)} %bitcast.88), calls=%async_computation.8 | async-start | bytes 8388608
  36.0 26.9 %copy-start.1 = (bf16[1,256,1024]{2,1,0:T(8,128)(2,1)S(1)}, bf16[1,256,1024]{2,1,0:T(8,128)(2,1)}, u32[]{:S(2)}) copy-start(bf16[1,256,1024]{2,1,0:T(8,128)(2,1)} %param.9) | copy-start | bytes 1572868
  42.0 82.6 %all-gather.4.cloned.1.call-start = ((), (), s32[]{:S(2)}) async-start(), calls=%async_computation.4 | async-start | bytes 4325376 | tf_op jit(solution)/shard_map/all_gather | solution.py:94
  64.5 12.0 %copy-start.2 = (bf16[1024,32]{0,1:T(8,128)(2,1)S(1)}, bf16[1024,32]{0,1:T(8,128)(2,1)}, u32[]{:S(2)}) copy-start(bf16[1024,32]{0,1:T(8,128)(2,1)} %param.6) | copy-start | bytes 196612
Sparse Core Ops, SparseCore 0:
  42.1 4.9 reduce-scatter.1
  64.6 59.9 all-gather.3
